TPU v7x, 32 devices: a whole 2x2x4 slice. The times are simulated.
32 devices in a mesh: dom: 8 (over z, y), rows: 4 (over x, core).
Axes of the slice: x: 2, y: 2, z: 4, core: 2. Of those that a mesh axis runs over, the one named last changes fastest.
Arguments:
- fields: float32 [8, 3, 128, 4096], P('dom', None, 'rows'), may hold values from -6 to 6
- depth: float32 [128, 4096], P('rows'), may hold values from 1.5 to 6
- obs_index: int32 [256], replicated, may hold values from 0 to 524287, as said below
- obs_value: float32 [256], replicated, may hold values from -6 to 6
- obs_var: float32 [256], replicated, may hold values from 0.5 to 5
- parent_lookup: int32 [8], replicated, may hold values from 0 to 7, as said below
Outputs:
- log_weights: float32 [8], P('dom')
- posterior_members: float32 [8, 3, 128, 4096], P('dom', None, 'rows')
Inputs may be any that keep to these rules, and one draw needn't show every extreme that they name: `parent_lookup`: every value is the index of a particle; 0 and 7 each appear; values may repeat. `obs_index`: indices of grid cells, possibly repeated; the first and last cell each appear.
All inputs are finite; a program needn't handle non-finite values.
Results may differ from a plain program's by a relative error of at most 0.00003.
Values sent between devices are 32-bit elements; how exact they have to be, the bound alone decides.
No kernel may reach another device: no remote copies, remote signals or barrier semaphores. Data moves between devices by JAX's collectives and lax.ppermute only.
A program may use at most 64 MiB of HBM per device.

v0:
```python
import jax
import jax.numpy as jnp
from jax import lax
from jax.sharding import PartitionSpec as P

STEPS = 4
time_step = 0.5
coriolis = 0.2


def extended(cells, sides, width):
    for axis, dim in sides:
        count = lax.axis_size(axis)
        ends = count - 1
        head = lax.slice_in_dim(cells, 0, width, axis=dim)
        tail = lax.slice_in_dim(cells, cells.shape[dim] - width, cells.shape[dim], axis=dim)
        cells = jnp.concatenate(
            [
                lax.ppermute(tail, axis, [(i, (i + 1) % count) for i in range(ends)]),
                cells,
                lax.ppermute(head, axis, [((i + 1) % count, i) for i in range(ends)]),
            ],
            axis=dim,
        )
    return cells


def cols_diff(a):
    return 0.5 * (jnp.roll(a, -1, axis=-1) - jnp.roll(a, 1, axis=-1))


def flux_rows_diff(a):
    padded = extended(a, (("rows", 1),), 1)
    return 0.5 * (padded[:, 2:] - padded[:, :-2])


def height_rows_diff(a):
    padded = extended(a, (("rows", 1),), 1)
    return 0.5 * (padded[:, 2:] - padded[:, :-2])


def shards(fields, depth, obs_index, obs_value, obs_var, parent_lookup):
    free_elevation = fields[:, 0]
    zonal_current = fields[:, 1]
    meridional_current = fields[:, 2]
    depth_rows = depth[None]
    for step in range(STEPS):
        free_elevation = free_elevation - time_step * (
            cols_diff(depth_rows * zonal_current) + flux_rows_diff(depth_rows * meridional_current)
        )
        zonal_current = (
            zonal_current
            - time_step * cols_diff(free_elevation)
            + time_step * coriolis * meridional_current
        )
        meridional_current = (
            meridional_current
            - time_step * height_rows_diff(free_elevation)
            - time_step * coriolis * zonal_current
        )
    prior_members = jnp.stack([free_elevation, zonal_current, meridional_current], axis=1)
    slab_cells = free_elevation.shape[1] * free_elevation.shape[2]
    flat = free_elevation.reshape(free_elevation.shape[0], slab_cells)
    offset = obs_index - lax.axis_index("rows") * slab_cells
    inside = (offset >= 0) & (offset < slab_cells)
    values = jnp.take(flat, jnp.clip(offset, 0, slab_cells - 1), axis=1)
    misfit = jnp.where(inside[None, :], (obs_value[None, :] - values) ** 2 / obs_var[None, :], 0.0)
    loglik = lax.psum(-0.5 * jnp.sum(misfit, axis=1), "rows")
    local_peak = jnp.max(loglik)
    peak = lax.pmax(local_peak, "dom")
    total = lax.psum(jnp.sum(jnp.exp(loglik - peak)), "dom")
    log_weights = loglik - (peak + jnp.log(total))
    member_batches = lax.axis_size("dom")
    subregion_tiles = prior_members.reshape(prior_members.shape[0], member_batches, -1)
    received = lax.all_to_all(subregion_tiles, "dom", split_axis=1, concat_axis=0, tiled=True)
    picked = jnp.take(received, parent_lookup, axis=0)
    final_answer = lax.all_to_all(picked, "dom", split_axis=0, concat_axis=1, tiled=True)
    posterior_members = final_answer.reshape(prior_members.shape)
    return (log_weights, posterior_members)


def solution(mesh):
    in_specs = (P("dom", None, "rows", None), P("rows", None), P(), P(), P(), P())
    out_specs = (P("dom"), P("dom", None, "rows", None))
    return jax.shard_map(shards, mesh=mesh, in_specs=in_specs, out_specs=out_specs, check_vma=False)
```

profile of v0, /device:TPU:0, one launch (start us, length us, event | category | flops | bytes accessed | tf_op | source)
XLA Modules:
  0.0 196.9 jit_solution(10956344238698657955)
XLA Ops:
  0.6 1.5 fusion.51
  2.1 1.4 collective-permute-start
  3.6 3.0 %collective-permute-start.1 = (f32[1,1,4096]{2,1,0:T(1,128)S(1)}, f32[1,1,4096]{2,1,0:T(1,128)S(1)}, u32[]{:S(2)}, u32[]{:S(2)}) collective-permute-start(f32[1,1,4096]{2,1,0:T(1,128)S(1)} %get-tuple-element.68), channel_id=1, source_target_pairs={{0,1},{1,2},{2,3},{4,5},{5,6},{6,7},{8,9},{9,10},{10,11},{12,13},{... | collective-permute-start | bytes 49160 | tf_op jit(solution)/shard_map/ppermute | solution.py:19
  8.0 1.3 collective-permute-start.2
  9.3 5.1 %collective-permute-start.3 = (f32[1,1,4096]{2,1,0:T(1,128)S(1)}, f32[1,1,4096]{2,1,0:T(1,128)S(1)}, u32[]{:S(2)}, u32[]{:S(2)}) collective-permute-start(f32[1,1,4096]{2,1,0:T(1,128)S(1)} %get-tuple-element.62), channel_id=1, source_target_pairs={{0,1},{1,2},{2,3},{4,5},{5,6},{6,7},{8,9},{9,10},{10,11},{12,13},{... | collective-permute-start | bytes 49160 | tf_op jit(solution)/shard_map/ppermute | solution.py:19
  15.7 1.3 collective-permute-start.4
  17.0 4.9 %collective-permute-start.5 = (f32[1,1,4096]{2,1,0:T(1,128)S(1)}, f32[1,1,4096]{2,1,0:T(1,128)S(1)}, u32[]{:S(2)}, u32[]{:S(2)}) collective-permute-start(f32[1,1,4096]{2,1,0:T(1,128)S(1)} %get-tuple-element.60), channel_id=1, source_target_pairs={{0,1},{1,2},{2,3},{4,5},{5,6},{6,7},{8,9},{9,10},{10,11},{12,13},{... | collective-permute-start | bytes 49160 | tf_op jit(solution)/shard_map/ppermute | solution.py:19
  21.9 0.7 collective-permute-done.5
  23.2 1.3 collective-permute-start.6
  24.5 4.9 %collective-permute-start.7 = (f32[1,1,4096]{2,1,0:T(1,128)S(1)}, f32[1,1,4096]{2,1,0:T(1,128)S(1)}, u32[]{:S(2)}, u32[]{:S(2)}) collective-permute-start(f32[1,1,4096]{2,1,0:T(1,128)S(1)} %get-tuple-element.42), channel_id=1, source_target_pairs={{0,1},{1,2},{2,3},{4,5},{5,6},{6,7},{8,9},{9,10},{10,11},{12,13},{... | collective-permute-start | bytes 49160 | tf_op jit(solution)/shard_map/ppermute | solution.py:19
  30.4 1.3 collective-permute-start.8
  31.7 4.9 %collective-permute-start.9 = (f32[1,1,4096]{2,1,0:T(1,128)S(1)}, f32[1,1,4096]{2,1,0:T(1,128)S(1)}, u32[]{:S(2)}, u32[]{:S(2)}) collective-permute-start(f32[1,1,4096]{2,1,0:T(1,128)S(1)} %get-tuple-element.40), channel_id=1, source_target_pairs={{0,1},{1,2},{2,3},{4,5},{5,6},{6,7},{8,9},{9,10},{10,11},{12,13},{... | collective-permute-start | bytes 49160 | tf_op jit(solution)/shard_map/ppermute | solution.py:19
  38.0 1.3 collective-permute-start.10
  39.3 4.9 %collective-permute-start.11 = (f32[1,1,4096]{2,1,0:T(1,128)S(1)}, f32[1,1,4096]{2,1,0:T(1,128)S(1)}, u32[]{:S(2)}, u32[]{:S(2)}) collective-permute-start(f32[1,1,4096]{2,1,0:T(1,128)S(1)} %get-tuple-element.30), channel_id=1, source_target_pairs={{0,1},{1,2},{2,3},{4,5},{5,6},{6,7},{8,9},{9,10},{10,11},{12,13},{... | collective-permute-start | bytes 49160 | tf_op jit(solution)/shard_map/ppermute | solution.py:19
  45.2 1.3 collective-permute-start.12
  46.5 4.9 %collective-permute-start.13 = (f32[1,1,4096]{2,1,0:T(1,128)S(1)}, f32[1,1,4096]{2,1,0:T(1,128)S(1)}, u32[]{:S(2)}, u32[]{:S(2)}) collective-permute-start(f32[1,1,4096]{2,1,0:T(1,128)S(1)} %get-tuple-element.28), channel_id=1, source_target_pairs={{0,1},{1,2},{2,3},{4,5},{5,6},{6,7},{8,9},{9,10},{10,11},{12,13},{... | collective-permute-start | bytes 49160 | tf_op jit(solution)/shard_map/ppermute | solution.py:19
  52.7 1.3 collective-permute-start.14
  54.0 4.9 %collective-permute-start.15 = (f32[1,1,4096]{2,1,0:T(1,128)S(1)}, f32[1,1,4096]{2,1,0:T(1,128)S(1)}, u32[]{:S(2)}, u32[]{:S(2)}) collective-permute-start(f32[1,1,4096]{2,1,0:T(1,128)S(1)} %get-tuple-element.22), channel_id=1, source_target_pairs={{0,1},{1,2},{2,3},{4,5},{5,6},{6,7},{8,9},{9,10},{10,11},{12,13},{... | collective-permute-start | bytes 49160 | tf_op jit(solution)/shard_map/ppermute | solution.py:19
  60.2 2.8 %reshape.582 = f32[1,8,49152]{2,0,1:T(1,128)} reshape(f32[1,3,32,4096]{3,2,1,0:T(8,128)S(1)} %pad_maximum_fusion) | data formatting | bytes 3145728 | tf_op jit(solution)/shard_map/reshape | solution.py:74
  63.0 6.0 %all-to-all-start = ((f32[1,8,49152]{2,0,1:T(1,128)}), f32[1,8,49152]{2,0,1:T(1,128)}, u32[]{:S(2)}, u32[]{:S(2)}) async-start(f32[1,8,49152]{2,0,1:T(1,128)} %reshape.582), calls=%async_computation | async-start | bytes 3145728 | tf_op jit(solution)/shard_map/all_to_all | solution.py:75
  69.0 37.9 %all-to-all-done = f32[1,8,49152]{2,0,1:T(1,128)} async-done(((f32[1,8,49152]{2,0,1:T(1,128)}), f32[1,8,49152]{2,0,1:T(1,128)}, u32[]{:S(2)}, u32[]{:S(2)}) %all-to-all-start) | async-done | bytes 1572896 | tf_op jit(solution)/shard_map/all_to_all | solution.py:75
  106.9 2.3 %copy.18 = f32[1,8,49152]{2,1,0:T(8,128)S(1)} copy(f32[1,8,49152]{2,0,1:T(1,128)} %all-to-all-done) | data formatting | bytes 3145728
  109.2 2.1 %gather_fusion.1 = f32[8,49152]{1,0:T(8,128)} fusion(f32[8,49152]{1,0:T(8,128)S(1)} %bitcast.62, s32[1024]{0:T(1024)S(1)} %pad_clamp_fusion), kind=kCustom, calls=%fused_computation.1 | custom fusion | bytes 3145760 | tf_op jit(solution)/shard_map/jit(_take)/gather | solution.py:76
  111.3 1.6 bitcast_select_fusion
  112.9 2.8 %copy.14 = f32[8,1,49152]{2,1,0:T(1,128)} copy(f32[8,1,49152]{2,0,1:T(8,128)S(1)} %bitcast_select_fusion) | data formatting | bytes 3145728 | tf_op jit(solution)/shard_map/jit(_take)/select_n | solution.py:76
  115.6 4.3 %all-to-all-start.1 = ((f32[8,1,49152]{2,1,0:T(1,128)}), f32[8,1,49152]{2,1,0:T(1,128)S(1)}, u32[]{:S(2)}, u32[]{:S(2)}) async-start(f32[8,1,49152]{2,1,0:T(1,128)} %copy.14), calls=%async_computation.1 | async-start | bytes 3145728 | tf_op jit(solution)/shard_map/all_to_all | solution.py:77
  120.1 1.7 gather_fusion
  123.1 8.1 %psum.14 = f32[1]{0:T(128)} all-reduce(f32[1]{0:T(128)} %bitcast.13), channel_id=1, replica_groups=mesh['dom'=8,'rows'=4] {'rows'}, use_global_device_ids=true, to_apply=%region_1.2 | all-reduce | flops 1 | bytes 8 | tf_op jit(solution)/shard_map/psum | solution.py:68
  131.1 31.7 %pmax.7 = f32[]{:T(128)} all-reduce(f32[]{:T(128)} %bitcast.14), channel_id=1, replica_groups=mesh['dom'=8,'rows'=4] {'dom'}, use_global_device_ids=true, to_apply=%region_2.3 | all-reduce | flops 1 | bytes 8 | tf_op jit(solution)/shard_map/pmax | solution.py:70
  164.2 24.4 %psum.15 = f32[]{:T(128)} all-reduce(f32[]{:T(128)} %bitcast.16), channel_id=1, replica_groups=mesh['dom'=8,'rows'=4] {'dom'}, use_global_device_ids=true, to_apply=%region_3.4 | all-reduce | flops 1 | bytes 8 | tf_op jit(solution)/shard_map/psum | solution.py:71
  190.5 3.7 %reduce.2 = f32[8,49152]{1,0:T(8,128)S(1)} reduce(f32[8,1,49152]{2,1,0:T(1,128)S(1)} %all-to-all-done.1, f32[]{:T(128)} %constant.62), dimensions={1}, to_apply=%all_to_all.8.reduce_sub_computation | reduce | bytes 3145732 | tf_op jit(solution)/shard_map/all_to_all | solution.py:77
  194.2 1.6 reshape.583
  (71 shorter events, 10.1 us)
Async XLA Ops:
  2.1 5.3 %copy-start.1 = (f32[1,3,32,4096]{3,2,1,0:T(8,128)S(1)}, f32[1,3,32,4096]{3,2,1,0:T(8,128)}, u32[]{:S(2)}) copy-start(f32[1,3,32,4096]{3,2,1,0:T(8,128)} %param.6) | copy-start | bytes 4718596
  2.1 4.7 %collective-permute-start = (f32[1,1,4096]{2,1,0:T(1,128)S(1)}, f32[1,1,4096]{2,1,0:T(1,128)S(1)}, u32[]{:S(2)}, u32[]{:S(2)}) collective-permute-start(f32[1,1,4096]{2,1,0:T(1,128)S(1)} %get-tuple-element.67), channel_id=1, source_target_pairs={{1,0},{2,1},{3,2},{5,4},{6,5},{7,6},{9,8},{10,9},{11,10},{13,12},{... | collective-permute-start | bytes 49160 | tf_op jit(solution)/shard_map/ppermute | solution.py:21
  3.6 3.9 %collective-permute-start.1 = (f32[1,1,4096]{2,1,0:T(1,128)S(1)}, f32[1,1,4096]{2,1,0:T(1,128)S(1)}, u32[]{:S(2)}, u32[]{:S(2)}) collective-permute-start(f32[1,1,4096]{2,1,0:T(1,128)S(1)} %get-tuple-element.68), channel_id=1, source_target_pairs={{0,1},{1,2},{2,3},{4,5},{5,6},{6,7},{8,9},{9,10},{10,11},{12,13},{... | collective-permute-start | bytes 49160 | tf_op jit(solution)/shard_map/ppermute | solution.py:19
  7.8 6.7 %copy-start = (f32[32,4096]{1,0:T(8,128)S(1)}, f32[32,4096]{1,0:T(8,128)}, u32[]{:S(2)}) copy-start(f32[32,4096]{1,0:T(8,128)} %param.7) | copy-start | bytes 1572868
  8.0 6.9 %collective-permute-start.2 = (f32[1,1,4096]{2,1,0:T(1,128)S(1)}, f32[1,1,4096]{2,1,0:T(1,128)S(1)}, u32[]{:S(2)}, u32[]{:S(2)}) collective-permute-start(f32[1,1,4096]{2,1,0:T(1,128)S(1)} %get-tuple-element.61), channel_id=1, source_target_pairs={{1,0},{2,1},{3,2},{5,4},{6,5},{7,6},{9,8},{10,9},{11,10},{13,12},{... | collective-permute-start | bytes 49160 | tf_op jit(solution)/shard_map/ppermute | solution.py:21
  9.3 5.9 %collective-permute-start.3 = (f32[1,1,4096]{2,1,0:T(1,128)S(1)}, f32[1,1,4096]{2,1,0:T(1,128)S(1)}, u32[]{:S(2)}, u32[]{:S(2)}) collective-permute-start(f32[1,1,4096]{2,1,0:T(1,128)S(1)} %get-tuple-element.62), channel_id=1, source_target_pairs={{0,1},{1,2},{2,3},{4,5},{5,6},{6,7},{8,9},{9,10},{10,11},{12,13},{... | collective-permute-start | bytes 49160 | tf_op jit(solution)/shard_map/ppermute | solution.py:19
  15.7 6.2 %collective-permute-start.4 = (f32[1,1,4096]{2,1,0:T(1,128)S(1)}, f32[1,1,4096]{2,1,0:T(1,128)S(1)}, u32[]{:S(2)}, u32[]{:S(2)}) collective-permute-start(f32[1,1,4096]{2,1,0:T(1,128)S(1)} %get-tuple-element.59), channel_id=1, source_target_pairs={{1,0},{2,1},{3,2},{5,4},{6,5},{7,6},{9,8},{10,9},{11,10},{13,12},{... | collective-permute-start | bytes 49160 | tf_op jit(solution)/shard_map/ppermute | solution.py:21
  17.0 5.7 %collective-permute-start.5 = (f32[1,1,4096]{2,1,0:T(1,128)S(1)}, f32[1,1,4096]{2,1,0:T(1,128)S(1)}, u32[]{:S(2)}, u32[]{:S(2)}) collective-permute-start(f32[1,1,4096]{2,1,0:T(1,128)S(1)} %get-tuple-element.60), channel_id=1, source_target_pairs={{0,1},{1,2},{2,3},{4,5},{5,6},{6,7},{8,9},{9,10},{10,11},{12,13},{... | collective-permute-start | bytes 49160 | tf_op jit(solution)/shard_map/ppermute | solution.py:19
  23.2 6.6 %collective-permute-start.6 = (f32[1,1,4096]{2,1,0:T(1,128)S(1)}, f32[1,1,4096]{2,1,0:T(1,128)S(1)}, u32[]{:S(2)}, u32[]{:S(2)}) collective-permute-start(f32[1,1,4096]{2,1,0:T(1,128)S(1)} %get-tuple-element.41), channel_id=1, source_target_pairs={{1,0},{2,1},{3,2},{5,4},{6,5},{7,6},{9,8},{10,9},{11,10},{13,12},{... | collective-permute-start | bytes 49160 | tf_op jit(solution)/shard_map/ppermute | solution.py:21
  24.5 5.7 %collective-permute-start.7 = (f32[1,1,4096]{2,1,0:T(1,128)S(1)}, f32[1,1,4096]{2,1,0:T(1,128)S(1)}, u32[]{:S(2)}, u32[]{:S(2)}) collective-permute-start(f32[1,1,4096]{2,1,0:T(1,128)S(1)} %get-tuple-element.42), channel_id=1, source_target_pairs={{0,1},{1,2},{2,3},{4,5},{5,6},{6,7},{8,9},{9,10},{10,11},{12,13},{... | collective-permute-start | bytes 49160 | tf_op jit(solution)/shard_map/ppermute | solution.py:19
  30.4 6.2 %collective-permute-start.8 = (f32[1,1,4096]{2,1,0:T(1,128)S(1)}, f32[1,1,4096]{2,1,0:T(1,128)S(1)}, u32[]{:S(2)}, u32[]{:S(2)}) collective-permute-start(f32[1,1,4096]{2,1,0:T(1,128)S(1)} %get-tuple-element.39), channel_id=1, source_target_pairs={{1,0},{2,1},{3,2},{5,4},{6,5},{7,6},{9,8},{10,9},{11,10},{13,12},{... | collective-permute-start | bytes 49160 | tf_op jit(solution)/shard_map/ppermute | solution.py:21
  31.7 5.7 %collective-permute-start.9 = (f32[1,1,4096]{2,1,0:T(1,128)S(1)}, f32[1,1,4096]{2,1,0:T(1,128)S(1)}, u32[]{:S(2)}, u32[]{:S(2)}) collective-permute-start(f32[1,1,4096]{2,1,0:T(1,128)S(1)} %get-tuple-element.40), channel_id=1, source_target_pairs={{0,1},{1,2},{2,3},{4,5},{5,6},{6,7},{8,9},{9,10},{10,11},{12,13},{... | collective-permute-start | bytes 49160 | tf_op jit(solution)/shard_map/ppermute | solution.py:19
  38.0 6.6 %collective-permute-start.10 = (f32[1,1,4096]{2,1,0:T(1,128)S(1)}, f32[1,1,4096]{2,1,0:T(1,128)S(1)}, u32[]{:S(2)}, u32[]{:S(2)}) collective-permute-start(f32[1,1,4096]{2,1,0:T(1,128)S(1)} %get-tuple-element.29), channel_id=1, source_target_pairs={{1,0},{2,1},{3,2},{5,4},{6,5},{7,6},{9,8},{10,9},{11,10},{13,12},{... | collective-permute-start | bytes 49160 | tf_op jit(solution)/shard_map/ppermute | solution.py:21
  39.3 5.7 %collective-permute-start.11 = (f32[1,1,4096]{2,1,0:T(1,128)S(1)}, f32[1,1,4096]{2,1,0:T(1,128)S(1)}, u32[]{:S(2)}, u32[]{:S(2)}) collective-permute-start(f32[1,1,4096]{2,1,0:T(1,128)S(1)} %get-tuple-element.30), channel_id=1, source_target_pairs={{0,1},{1,2},{2,3},{4,5},{5,6},{6,7},{8,9},{9,10},{10,11},{12,13},{... | collective-permute-start | bytes 49160 | tf_op jit(solution)/shard_map/ppermute | solution.py:19
  45.2 6.2 %collective-permute-start.12 = (f32[1,1,4096]{2,1,0:T(1,128)S(1)}, f32[1,1,4096]{2,1,0:T(1,128)S(1)}, u32[]{:S(2)}, u32[]{:S(2)}) collective-permute-start(f32[1,1,4096]{2,1,0:T(1,128)S(1)} %get-tuple-element.27), channel_id=1, source_target_pairs={{1,0},{2,1},{3,2},{5,4},{6,5},{7,6},{9,8},{10,9},{11,10},{13,12},{... | collective-permute-start | bytes 49160 | tf_op jit(solution)/shard_map/ppermute | solution.py:21
  46.5 5.7 %collective-permute-start.13 = (f32[1,1,4096]{2,1,0:T(1,128)S(1)}, f32[1,1,4096]{2,1,0:T(1,128)S(1)}, u32[]{:S(2)}, u32[]{:S(2)}) collective-permute-start(f32[1,1,4096]{2,1,0:T(1,128)S(1)} %get-tuple-element.28), channel_id=1, source_target_pairs={{0,1},{1,2},{2,3},{4,5},{5,6},{6,7},{8,9},{9,10},{10,11},{12,13},{... | collective-permute-start | bytes 49160 | tf_op jit(solution)/shard_map/ppermute | solution.py:19
  52.7 6.2 %collective-permute-start.14 = (f32[1,1,4096]{2,1,0:T(1,128)S(1)}, f32[1,1,4096]{2,1,0:T(1,128)S(1)}, u32[]{:S(2)}, u32[]{:S(2)}) collective-permute-start(f32[1,1,4096]{2,1,0:T(1,128)S(1)} %get-tuple-element.21), channel_id=1, source_target_pairs={{1,0},{2,1},{3,2},{5,4},{6,5},{7,6},{9,8},{10,9},{11,10},{13,12},{... | collective-permute-start | bytes 49160 | tf_op jit(solution)/shard_map/ppermute | solution.py:21
  54.0 5.7 %collective-permute-start.15 = (f32[1,1,4096]{2,1,0:T(1,128)S(1)}, f32[1,1,4096]{2,1,0:T(1,128)S(1)}, u32[]{:S(2)}, u32[]{:S(2)}) collective-permute-start(f32[1,1,4096]{2,1,0:T(1,128)S(1)} %get-tuple-element.22), channel_id=1, source_target_pairs={{0,1},{1,2},{2,3},{4,5},{5,6},{6,7},{8,9},{9,10},{10,11},{12,13},{... | collective-permute-start | bytes 49160 | tf_op jit(solution)/shard_map/ppermute | solution.py:19
  63.0 6.0 %copy-start.5 = (s32[8]{0:T(128)S(1)}, s32[8]{0:T(128)}, u32[]{:S(2)}) copy-start(s32[8]{0:T(128)} %param.11) | copy-start | bytes 100
  63.0 43.9 %all-to-all-start = ((f32[1,8,49152]{2,0,1:T(1,128)}), f32[1,8,49152]{2,0,1:T(1,128)}, u32[]{:S(2)}, u32[]{:S(2)}) async-start(f32[1,8,49152]{2,0,1:T(1,128)} %reshape.582), calls=%async_computation | async-start | bytes 3145728 | tf_op jit(solution)/shard_map/all_to_all | solution.py:75
  115.6 4.3 %copy-start.2 = (s32[256]{0:T(256)S(1)}, s32[256]{0:T(256)}, u32[]{:S(2)}) copy-start(s32[256]{0:T(256)} %param.8) | copy-start | bytes 3076
  115.6 74.8 %all-to-all-start.1 = ((f32[8,1,49152]{2,1,0:T(1,128)}), f32[8,1,49152]{2,1,0:T(1,128)S(1)}, u32[]{:S(2)}, u32[]{:S(2)}) async-start(f32[8,1,49152]{2,1,0:T(1,128)} %copy.14), calls=%async_computation.1 | async-start | bytes 3145728 | tf_op jit(solution)/shard_map/all_to_all | solution.py:77
  119.9 1.9 copy-start.3
  119.9 1.9 copy-start.4
where the time goes:
time: 198 us; the launch traced here: 197 us
  blocking collectives  64.2 us (32%)
  starting transfers between devices  58 us (29%)
  waiting for transfers between devices  42.5 us (21%)
  local copies, waits for them, and re-layouts  15.8 us (8%)
  other arithmetic  10.4 us (5%)
  between operations  5.97 us (3%)
    all_to_all x1, waiting for transfers between devices, shards(): lax.all_to_all(subregion_tiles, 'dom', split_axis=1, concat_axis=0, tiled...  37.9 us
    ppermute x8, starting transfers between devices, extended(): lax.ppermute(tail, axis, [(i, (i + 1) % count) for i in range(ends)])  37.3 us
    pmax x1, blocking collectives, shards(): peak = lax.pmax(local_peak, 'dom')  31.7 us
    psum x1, blocking collectives, shards(): total = lax.psum(jnp.sum(jnp.exp(loglik - peak)), 'dom')  24.4 us
    ppermute x8, starting transfers between devices, extended(): lax.ppermute(head, axis, [((i + 1) % count, i) for i in range(ends)])  10.5 us
    psum x1, blocking collectives, shards(): loglik = lax.psum(-0.5 * jnp.sum(misfit, axis=1), 'rows')  8.06 us
    all_to_all x1, starting transfers between devices, shards(): lax.all_to_all(subregion_tiles, 'dom', split_axis=1, concat_axis=0, tiled...  5.97 us
    ppermute x8, waiting for transfers between devices, extended(): lax.ppermute(tail, axis, [(i, (i + 1) % count) for i in range(ends)])  4.65 us
  transfers between devices with their start and end apart: 18, of which 9 were waited for; matrix products, arithmetic and copies ran while one was open for 2% of the time, Pallas kernels for 0%

commit v1 on v0

--- a/solution.py
+++ b/solution.py
@@ -6,6 +6,10 @@
 STEPS = 4
 time_step = 0.5
 coriolis = 0.2
+
+
+def time_cube(own_rows):
+    return jnp.sum(lax.all_gather(own_rows, "rows"), axis=0)
 
 
 def extended(cells, sides, width):
@@ -65,7 +69,7 @@
     inside = (offset >= 0) & (offset < slab_cells)
     values = jnp.take(flat, jnp.clip(offset, 0, slab_cells - 1), axis=1)
     misfit = jnp.where(inside[None, :], (obs_value[None, :] - values) ** 2 / obs_var[None, :], 0.0)
-    loglik = lax.psum(-0.5 * jnp.sum(misfit, axis=1), "rows")
+    loglik = time_cube(-0.5 * jnp.sum(misfit, axis=1))
     local_peak = jnp.max(loglik)
     peak = lax.pmax(local_peak, "dom")
     total = lax.psum(jnp.sum(jnp.exp(loglik - peak)), "dom")

time: 198 us -> 197 us (level)
  blocking collectives: 64.2 us -> 61.6 us
    psum x1 -> x0, blocking collectives: 8.06 us -> none  [shards(): loglik = lax.psum(-0.5 * jnp.sum(misfit, axis=1), 'rows')]
    unnamed x0 -> x1, blocking collectives: none -> 7.08 us
  transfers between devices with their start and end apart: 18 -> 18, of which waited for: 9 -> 9; matrix products, arithmetic and copies ran while one was open for 2% -> 3% of each run, Pallas kernels for 0% -> 0%
where the time goes in v1:
time: 197 us; the launch traced here: 196 us
  blocking collectives  61.6 us (31%)
  starting transfers between devices  58 us (29%)
  waiting for transfers between devices  42.5 us (22%)
  local copies, waits for them, and re-layouts  17.2 us (9%)
  other arithmetic  11 us (6%)
  between operations  6.08 us (3%)
    all_to_all x1, waiting for transfers between devices, shards(): lax.all_to_all(subregion_tiles, 'dom', split_axis=1, concat_axis=0, tiled...  37.9 us
    ppermute x8, starting transfers between devices, extended(): lax.ppermute(tail, axis, [(i, (i + 1) % count) for i in range(ends)])  37.3 us
    pmax x1, blocking collectives, shards(): peak = lax.pmax(local_peak, 'dom')  30.8 us
    psum x1, blocking collectives, shards(): total = lax.psum(jnp.sum(jnp.exp(loglik - peak)), 'dom')  23.8 us
    ppermute x8, starting transfers between devices, extended(): lax.ppermute(head, axis, [((i + 1) % count, i) for i in range(ends)])  10.5 us
    unnamed x1, blocking collectives  7.08 us
    all_to_all x1, starting transfers between devices, shards(): lax.all_to_all(subregion_tiles, 'dom', split_axis=1, concat_axis=0, tiled...  5.97 us
    ppermute x8, waiting for transfers between devices, extended(): lax.ppermute(tail, axis, [(i, (i + 1) % count) for i in range(ends)])  4.65 us
  transfers between devices with their start and end apart: 18, of which 9 were waited for; matrix products, arithmetic and copies ran while one was open for 3% of the time, Pallas kernels for 0%

profile of v1, /device:TPU:0, one launch (start us, length us, event | category | flops | bytes accessed | tf_op | source)
XLA Modules:
  0.0 196.4 jit_solution(10204052808866241028)
XLA Ops:
  0.6 1.5 fusion.51
  2.1 1.4 collective-permute-start
  3.6 3.0 %collective-permute-start.1 = (f32[1,1,4096]{2,1,0:T(1,128)S(1)}, f32[1,1,4096]{2,1,0:T(1,128)S(1)}, u32[]{:S(2)}, u32[]{:S(2)}) collective-permute-start(f32[1,1,4096]{2,1,0:T(1,128)S(1)} %get-tuple-element.68), channel_id=1, source_target_pairs={{0,1},{1,2},{2,3},{4,5},{5,6},{6,7},{8,9},{9,10},{10,11},{12,13},{... | collective-permute-start | bytes 49160 | tf_op jit(solution)/shard_map/ppermute | solution.py:23
  8.0 1.3 collective-permute-start.2
  9.3 5.1 %collective-permute-start.3 = (f32[1,1,4096]{2,1,0:T(1,128)S(1)}, f32[1,1,4096]{2,1,0:T(1,128)S(1)}, u32[]{:S(2)}, u32[]{:S(2)}) collective-permute-start(f32[1,1,4096]{2,1,0:T(1,128)S(1)} %get-tuple-element.62), channel_id=1, source_target_pairs={{0,1},{1,2},{2,3},{4,5},{5,6},{6,7},{8,9},{9,10},{10,11},{12,13},{... | collective-permute-start | bytes 49160 | tf_op jit(solution)/shard_map/ppermute | solution.py:23
  15.7 1.3 collective-permute-start.4
  17.0 4.9 %collective-permute-start.5 = (f32[1,1,4096]{2,1,0:T(1,128)S(1)}, f32[1,1,4096]{2,1,0:T(1,128)S(1)}, u32[]{:S(2)}, u32[]{:S(2)}) collective-permute-start(f32[1,1,4096]{2,1,0:T(1,128)S(1)} %get-tuple-element.60), channel_id=1, source_target_pairs={{0,1},{1,2},{2,3},{4,5},{5,6},{6,7},{8,9},{9,10},{10,11},{12,13},{... | collective-permute-start | bytes 49160 | tf_op jit(solution)/shard_map/ppermute | solution.py:23
  21.9 0.7 collective-permute-done.5
  23.2 1.3 collective-permute-start.6
  24.5 4.9 %collective-permute-start.7 = (f32[1,1,4096]{2,1,0:T(1,128)S(1)}, f32[1,1,4096]{2,1,0:T(1,128)S(1)}, u32[]{:S(2)}, u32[]{:S(2)}) collective-permute-start(f32[1,1,4096]{2,1,0:T(1,128)S(1)} %get-tuple-element.42), channel_id=1, source_target_pairs={{0,1},{1,2},{2,3},{4,5},{5,6},{6,7},{8,9},{9,10},{10,11},{12,13},{... | collective-permute-start | bytes 49160 | tf_op jit(solution)/shard_map/ppermute | solution.py:23
  30.4 1.3 collective-permute-start.8
  31.7 4.9 %collective-permute-start.9 = (f32[1,1,4096]{2,1,0:T(1,128)S(1)}, f32[1,1,4096]{2,1,0:T(1,128)S(1)}, u32[]{:S(2)}, u32[]{:S(2)}) collective-permute-start(f32[1,1,4096]{2,1,0:T(1,128)S(1)} %get-tuple-element.40), channel_id=1, source_target_pairs={{0,1},{1,2},{2,3},{4,5},{5,6},{6,7},{8,9},{9,10},{10,11},{12,13},{... | collective-permute-start | bytes 49160 | tf_op jit(solution)/shard_map/ppermute | solution.py:23
  38.0 1.3 collective-permute-start.10
  39.3 4.9 %collective-permute-start.11 = (f32[1,1,4096]{2,1,0:T(1,128)S(1)}, f32[1,1,4096]{2,1,0:T(1,128)S(1)}, u32[]{:S(2)}, u32[]{:S(2)}) collective-permute-start(f32[1,1,4096]{2,1,0:T(1,128)S(1)} %get-tuple-element.30), channel_id=1, source_target_pairs={{0,1},{1,2},{2,3},{4,5},{5,6},{6,7},{8,9},{9,10},{10,11},{12,13},{... | collective-permute-start | bytes 49160 | tf_op jit(solution)/shard_map/ppermute | solution.py:23
  45.2 1.3 collective-permute-start.12
  46.5 4.9 %collective-permute-start.13 = (f32[1,1,4096]{2,1,0:T(1,128)S(1)}, f32[1,1,4096]{2,1,0:T(1,128)S(1)}, u32[]{:S(2)}, u32[]{:S(2)}) collective-permute-start(f32[1,1,4096]{2,1,0:T(1,128)S(1)} %get-tuple-element.28), channel_id=1, source_target_pairs={{0,1},{1,2},{2,3},{4,5},{5,6},{6,7},{8,9},{9,10},{10,11},{12,13},{... | collective-permute-start | bytes 49160 | tf_op jit(solution)/shard_map/ppermute | solution.py:23
  52.7 1.3 collective-permute-start.14
  54.0 4.9 %collective-permute-start.15 = (f32[1,1,4096]{2,1,0:T(1,128)S(1)}, f32[1,1,4096]{2,1,0:T(1,128)S(1)}, u32[]{:S(2)}, u32[]{:S(2)}) collective-permute-start(f32[1,1,4096]{2,1,0:T(1,128)S(1)} %get-tuple-element.22), channel_id=1, source_target_pairs={{0,1},{1,2},{2,3},{4,5},{5,6},{6,7},{8,9},{9,10},{10,11},{12,13},{... | collective-permute-start | bytes 49160 | tf_op jit(solution)/shard_map/ppermute | solution.py:23
  60.2 2.8 %reshape.589 = f32[1,8,49152]{2,0,1:T(1,128)} reshape(f32[1,3,32,4096]{3,2,1,0:T(8,128)S(1)} %pad_maximum_fusion) | data formatting | bytes 3145728 | tf_op jit(solution)/shard_map/reshape | solution.py:78
  63.0 6.0 %all-to-all-start = ((f32[1,8,49152]{2,0,1:T(1,128)}), f32[1,8,49152]{2,0,1:T(1,128)}, u32[]{:S(2)}, u32[]{:S(2)}) async-start(f32[1,8,49152]{2,0,1:T(1,128)} %reshape.589), calls=%async_computation | async-start | bytes 3145728 | tf_op jit(solution)/shard_map/all_to_all | solution.py:79
  69.0 37.9 %all-to-all-done = f32[1,8,49152]{2,0,1:T(1,128)} async-done(((f32[1,8,49152]{2,0,1:T(1,128)}), f32[1,8,49152]{2,0,1:T(1,128)}, u32[]{:S(2)}, u32[]{:S(2)}) %all-to-all-start) | async-done | bytes 1572896 | tf_op jit(solution)/shard_map/all_to_all | solution.py:79
  106.9 2.3 %copy.18 = f32[1,8,49152]{2,1,0:T(8,128)S(1)} copy(f32[1,8,49152]{2,0,1:T(1,128)} %all-to-all-done) | data formatting | bytes 3145728
  109.2 2.1 %gather_fusion.1 = f32[8,49152]{1,0:T(8,128)} fusion(f32[8,49152]{1,0:T(8,128)S(1)} %bitcast.60, s32[1024]{0:T(1024)S(1)} %pad_clamp_fusion), kind=kCustom, calls=%fused_computation.1 | custom fusion | bytes 3145760 | tf_op jit(solution)/shard_map/jit(_take)/gather | solution.py:80
  111.3 1.6 bitcast_select_fusion
  112.9 2.8 %copy.14 = f32[8,1,49152]{2,1,0:T(1,128)} copy(f32[8,1,49152]{2,0,1:T(8,128)S(1)} %bitcast_select_fusion) | data formatting | bytes 3145728 | tf_op jit(solution)/shard_map/jit(_take)/select_n | solution.py:80
  115.6 4.3 %all-to-all-start.1 = ((f32[8,1,49152]{2,1,0:T(1,128)}), f32[8,1,49152]{2,1,0:T(1,128)S(1)}, u32[]{:S(2)}, u32[]{:S(2)}) async-start(f32[8,1,49152]{2,1,0:T(1,128)} %copy.14), calls=%async_computation.1 | async-start | bytes 3145728 | tf_op jit(solution)/shard_map/all_to_all | solution.py:81
  120.7 1.7 gather_fusion
  124.5 7.1 %all-reduce = f32[4]{0:T(128)S(1)} all-reduce(f32[4]{0:T(128)S(1)} %dynamic-update-slice), channel_id=1, replica_groups=mesh['dom'=8,'rows'=4] {'rows'}, use_global_device_ids=true, to_apply=%add | all-reduce | flops 4 | bytes 32
  132.1 30.8 %pmax.7 = f32[]{:T(128)} all-reduce(f32[]{:T(128)} %reduce.3), channel_id=1, replica_groups=mesh['dom'=8,'rows'=4] {'dom'}, use_global_device_ids=true, to_apply=%region_2.3 | all-reduce | flops 1 | bytes 8 | tf_op jit(solution)/shard_map/pmax | solution.py:74
  164.2 23.8 %psum.7 = f32[]{:T(128)} all-reduce(f32[]{:T(128)S(6)} %exp.4), channel_id=1, replica_groups=mesh['dom'=8,'rows'=4] {'dom'}, use_global_device_ids=true, to_apply=%region_3.4 | all-reduce | flops 1 | bytes 8 | tf_op jit(solution)/shard_map/psum | solution.py:75
  190.0 3.7 %reduce.5 = f32[8,49152]{1,0:T(8,128)S(1)} reduce(f32[8,1,49152]{2,1,0:T(1,128)S(1)} %all-to-all-done.1, f32[]{:T(128)} %constant.68), dimensions={1}, to_apply=%all_to_all.8.reduce_sub_computation | reduce | bytes 3145732 | tf_op jit(solution)/shard_map/all_to_all | solution.py:81
  193.7 1.6 reshape.590
  (77 shorter events, 12.1 us)
Async XLA Ops:
  2.1 5.3 %copy-start.1 = (f32[1,3,32,4096]{3,2,1,0:T(8,128)S(1)}, f32[1,3,32,4096]{3,2,1,0:T(8,128)}, u32[]{:S(2)}) copy-start(f32[1,3,32,4096]{3,2,1,0:T(8,128)} %param.6) | copy-start | bytes 4718596
  2.1 4.7 %collective-permute-start = (f32[1,1,4096]{2,1,0:T(1,128)S(1)}, f32[1,1,4096]{2,1,0:T(1,128)S(1)}, u32[]{:S(2)}, u32[]{:S(2)}) collective-permute-start(f32[1,1,4096]{2,1,0:T(1,128)S(1)} %get-tuple-element.67), channel_id=1, source_target_pairs={{1,0},{2,1},{3,2},{5,4},{6,5},{7,6},{9,8},{10,9},{11,10},{13,12},{... | collective-permute-start | bytes 49160 | tf_op jit(solution)/shard_map/ppermute | solution.py:25
  3.6 3.9 %collective-permute-start.1 = (f32[1,1,4096]{2,1,0:T(1,128)S(1)}, f32[1,1,4096]{2,1,0:T(1,128)S(1)}, u32[]{:S(2)}, u32[]{:S(2)}) collective-permute-start(f32[1,1,4096]{2,1,0:T(1,128)S(1)} %get-tuple-element.68), channel_id=1, source_target_pairs={{0,1},{1,2},{2,3},{4,5},{5,6},{6,7},{8,9},{9,10},{10,11},{12,13},{... | collective-permute-start | bytes 49160 | tf_op jit(solution)/shard_map/ppermute | solution.py:23
  7.8 6.7 %copy-start = (f32[32,4096]{1,0:T(8,128)S(1)}, f32[32,4096]{1,0:T(8,128)}, u32[]{:S(2)}) copy-start(f32[32,4096]{1,0:T(8,128)} %param.7) | copy-start | bytes 1572868
  8.0 6.9 %collective-permute-start.2 = (f32[1,1,4096]{2,1,0:T(1,128)S(1)}, f32[1,1,4096]{2,1,0:T(1,128)S(1)}, u32[]{:S(2)}, u32[]{:S(2)}) collective-permute-start(f32[1,1,4096]{2,1,0:T(1,128)S(1)} %get-tuple-element.61), channel_id=1, source_target_pairs={{1,0},{2,1},{3,2},{5,4},{6,5},{7,6},{9,8},{10,9},{11,10},{13,12},{... | collective-permute-start | bytes 49160 | tf_op jit(solution)/shard_map/ppermute | solution.py:25
  9.3 5.9 %collective-permute-start.3 = (f32[1,1,4096]{2,1,0:T(1,128)S(1)}, f32[1,1,4096]{2,1,0:T(1,128)S(1)}, u32[]{:S(2)}, u32[]{:S(2)}) collective-permute-start(f32[1,1,4096]{2,1,0:T(1,128)S(1)} %get-tuple-element.62), channel_id=1, source_target_pairs={{0,1},{1,2},{2,3},{4,5},{5,6},{6,7},{8,9},{9,10},{10,11},{12,13},{... | collective-permute-start | bytes 49160 | tf_op jit(solution)/shard_map/ppermute | solution.py:23
  15.7 6.2 %collective-permute-start.4 = (f32[1,1,4096]{2,1,0:T(1,128)S(1)}, f32[1,1,4096]{2,1,0:T(1,128)S(1)}, u32[]{:S(2)}, u32[]{:S(2)}) collective-permute-start(f32[1,1,4096]{2,1,0:T(1,128)S(1)} %get-tuple-element.59), channel_id=1, source_target_pairs={{1,0},{2,1},{3,2},{5,4},{6,5},{7,6},{9,8},{10,9},{11,10},{13,12},{... | collective-permute-start | bytes 49160 | tf_op jit(solution)/shard_map/ppermute | solution.py:25
  17.0 5.7 %collective-permute-start.5 = (f32[1,1,4096]{2,1,0:T(1,128)S(1)}, f32[1,1,4096]{2,1,0:T(1,128)S(1)}, u32[]{:S(2)}, u32[]{:S(2)}) collective-permute-start(f32[1,1,4096]{2,1,0:T(1,128)S(1)} %get-tuple-element.60), channel_id=1, source_target_pairs={{0,1},{1,2},{2,3},{4,5},{5,6},{6,7},{8,9},{9,10},{10,11},{12,13},{... | collective-permute-start | bytes 49160 | tf_op jit(solution)/shard_map/ppermute | solution.py:23
  23.2 6.6 %collective-permute-start.6 = (f32[1,1,4096]{2,1,0:T(1,128)S(1)}, f32[1,1,4096]{2,1,0:T(1,128)S(1)}, u32[]{:S(2)}, u32[]{:S(2)}) collective-permute-start(f32[1,1,4096]{2,1,0:T(1,128)S(1)} %get-tuple-element.41), channel_id=1, source_target_pairs={{1,0},{2,1},{3,2},{5,4},{6,5},{7,6},{9,8},{10,9},{11,10},{13,12},{... | collective-permute-start | bytes 49160 | tf_op jit(solution)/shard_map/ppermute | solution.py:25
  24.5 5.7 %collective-permute-start.7 = (f32[1,1,4096]{2,1,0:T(1,128)S(1)}, f32[1,1,4096]{2,1,0:T(1,128)S(1)}, u32[]{:S(2)}, u32[]{:S(2)}) collective-permute-start(f32[1,1,4096]{2,1,0:T(1,128)S(1)} %get-tuple-element.42), channel_id=1, source_target_pairs={{0,1},{1,2},{2,3},{4,5},{5,6},{6,7},{8,9},{9,10},{10,11},{12,13},{... | collective-permute-start | bytes 49160 | tf_op jit(solution)/shard_map/ppermute | solution.py:23
  30.4 6.2 %collective-permute-start.8 = (f32[1,1,4096]{2,1,0:T(1,128)S(1)}, f32[1,1,4096]{2,1,0:T(1,128)S(1)}, u32[]{:S(2)}, u32[]{:S(2)}) collective-permute-start(f32[1,1,4096]{2,1,0:T(1,128)S(1)} %get-tuple-element.39), channel_id=1, source_target_pairs={{1,0},{2,1},{3,2},{5,4},{6,5},{7,6},{9,8},{10,9},{11,10},{13,12},{... | collective-permute-start | bytes 49160 | tf_op jit(solution)/shard_map/ppermute | solution.py:25
  31.7 5.7 %collective-permute-start.9 = (f32[1,1,4096]{2,1,0:T(1,128)S(1)}, f32[1,1,4096]{2,1,0:T(1,128)S(1)}, u32[]{:S(2)}, u32[]{:S(2)}) collective-permute-start(f32[1,1,4096]{2,1,0:T(1,128)S(1)} %get-tuple-element.40), channel_id=1, source_target_pairs={{0,1},{1,2},{2,3},{4,5},{5,6},{6,7},{8,9},{9,10},{10,11},{12,13},{... | collective-permute-start | bytes 49160 | tf_op jit(solution)/shard_map/ppermute | solution.py:23
  38.0 6.6 %collective-permute-start.10 = (f32[1,1,4096]{2,1,0:T(1,128)S(1)}, f32[1,1,4096]{2,1,0:T(1,128)S(1)}, u32[]{:S(2)}, u32[]{:S(2)}) collective-permute-start(f32[1,1,4096]{2,1,0:T(1,128)S(1)} %get-tuple-element.29), channel_id=1, source_target_pairs={{1,0},{2,1},{3,2},{5,4},{6,5},{7,6},{9,8},{10,9},{11,10},{13,12},{... | collective-permute-start | bytes 49160 | tf_op jit(solution)/shard_map/ppermute | solution.py:25
  39.3 5.7 %collective-permute-start.11 = (f32[1,1,4096]{2,1,0:T(1,128)S(1)}, f32[1,1,4096]{2,1,0:T(1,128)S(1)}, u32[]{:S(2)}, u32[]{:S(2)}) collective-permute-start(f32[1,1,4096]{2,1,0:T(1,128)S(1)} %get-tuple-element.30), channel_id=1, source_target_pairs={{0,1},{1,2},{2,3},{4,5},{5,6},{6,7},{8,9},{9,10},{10,11},{12,13},{... | collective-permute-start | bytes 49160 | tf_op jit(solution)/shard_map/ppermute | solution.py:23
  45.2 6.2 %collective-permute-start.12 = (f32[1,1,4096]{2,1,0:T(1,128)S(1)}, f32[1,1,4096]{2,1,0:T(1,128)S(1)}, u32[]{:S(2)}, u32[]{:S(2)}) collective-permute-start(f32[1,1,4096]{2,1,0:T(1,128)S(1)} %get-tuple-element.27), channel_id=1, source_target_pairs={{1,0},{2,1},{3,2},{5,4},{6,5},{7,6},{9,8},{10,9},{11,10},{13,12},{... | collective-permute-start | bytes 49160 | tf_op jit(solution)/shard_map/ppermute | solution.py:25
  46.5 5.7 %collective-permute-start.13 = (f32[1,1,4096]{2,1,0:T(1,128)S(1)}, f32[1,1,4096]{2,1,0:T(1,128)S(1)}, u32[]{:S(2)}, u32[]{:S(2)}) collective-permute-start(f32[1,1,4096]{2,1,0:T(1,128)S(1)} %get-tuple-element.28), channel_id=1, source_target_pairs={{0,1},{1,2},{2,3},{4,5},{5,6},{6,7},{8,9},{9,10},{10,11},{12,13},{... | collective-permute-start | bytes 49160 | tf_op jit(solution)/shard_map/ppermute | solution.py:23
  52.7 6.2 %collective-permute-start.14 = (f32[1,1,4096]{2,1,0:T(1,128)S(1)}, f32[1,1,4096]{2,1,0:T(1,128)S(1)}, u32[]{:S(2)}, u32[]{:S(2)}) collective-permute-start(f32[1,1,4096]{2,1,0:T(1,128)S(1)} %get-tuple-element.21), channel_id=1, source_target_pairs={{1,0},{2,1},{3,2},{5,4},{6,5},{7,6},{9,8},{10,9},{11,10},{13,12},{... | collective-permute-start | bytes 49160 | tf_op jit(solution)/shard_map/ppermute | solution.py:25
  54.0 5.7 %collective-permute-start.15 = (f32[1,1,4096]{2,1,0:T(1,128)S(1)}, f32[1,1,4096]{2,1,0:T(1,128)S(1)}, u32[]{:S(2)}, u32[]{:S(2)}) collective-permute-start(f32[1,1,4096]{2,1,0:T(1,128)S(1)} %get-tuple-element.22), channel_id=1, source_target_pairs={{0,1},{1,2},{2,3},{4,5},{5,6},{6,7},{8,9},{9,10},{10,11},{12,13},{... | collective-permute-start | bytes 49160 | tf_op jit(solution)/shard_map/ppermute | solution.py:23
  63.0 6.0 %copy-start.5 = (s32[8]{0:T(128)S(1)}, s32[8]{0:T(128)}, u32[]{:S(2)}) copy-start(s32[8]{0:T(128)} %param.11) | copy-start | bytes 100
  63.0 43.9 %all-to-all-start = ((f32[1,8,49152]{2,0,1:T(1,128)}), f32[1,8,49152]{2,0,1:T(1,128)}, u32[]{:S(2)}, u32[]{:S(2)}) async-start(f32[1,8,49152]{2,0,1:T(1,128)} %reshape.589), calls=%async_computation | async-start | bytes 3145728 | tf_op jit(solution)/shard_map/all_to_all | solution.py:79
  115.6 4.3 %copy-start.6 = (u32[32]{0:T(128)S(1)}, u32[32]{0:T(128)}, u32[]{:S(2)}) copy-start(u32[32]{0:T(128)} %constant.64) | copy-start | bytes 388
  115.6 5.0 %copy-start.2 = (s32[256]{0:T(256)S(1)}, s32[256]{0:T(256)}, u32[]{:S(2)}) copy-start(s32[256]{0:T(256)} %param.8) | copy-start | bytes 3076
  115.6 74.3 %all-to-all-start.1 = ((f32[8,1,49152]{2,1,0:T(1,128)}), f32[8,1,49152]{2,1,0:T(1,128)S(1)}, u32[]{:S(2)}, u32[]{:S(2)}) async-start(f32[8,1,49152]{2,1,0:T(1,128)} %copy.14), calls=%async_computation.1 | async-start | bytes 3145728 | tf_op jit(solution)/shard_map/all_to_all | solution.py:81
  119.9 2.5 %copy-start.3 = (f32[256]{0:T(256)S(1)}, f32[256]{0:T(256)}, u32[]{:S(2)}) copy-start(f32[256]{0:T(256)} %param.10) | copy-start | bytes 3076
  119.9 2.5 %copy-start.4 = (f32[256]{0:T(256)S(1)}, f32[256]{0:T(256)}, u32[]{:S(2)}) copy-start(f32[256]{0:T(256)} %param.9) | copy-start | bytes 3076
